TPU v7x, 32 devices: a whole 2x2x4 slice. The times are simulated.
32 devices in a mesh: batch: 8 (over y, x, core), mp: 4 (over z).
Axes of the slice: x: 2, y: 2, z: 4, core: 2. Of those that a mesh axis runs over, the one named last changes fastest.
Arguments:
- token_ids: int32 [8, 1536], P('batch'), may hold values from 0 to 30527
- segment_ids: int32 [8, 1536], P('batch'), may hold values from 0 to 8, never falling along the last dimension, each value on 1 to 1024 neighbouring positions
- row_of: int32 [30528], replicated, may hold values from 0 to 30527, each once
- query_count: int32 [1], replicated, may hold values from 16 to 32
- table: float32 [30528, 768], P('batch'), may hold values from -8 to 8
- qkv_weight: float32 [768, 3, 768], P('batch', None, 'mp'), may hold values from -0.21875 to 0.21875
- out_weight: float32 [768, 768], P('mp', 'batch'), may hold values from -0.875 to 0.875
- gate_up_weight: float32 [768, 2, 3072], P('batch', None, 'mp'), may hold values from -0.21875 to 0.21875
- down_weight: float32 [3072, 768], P('mp', 'batch'), may hold values from -0.109375 to 0.109375
- gains: float32 [2, 768], P(None, 'batch'), may hold values from 0.3 to 2.5
- table_m: float32 [30528, 768], P('batch'), may hold values from -0.0009765625 to 0.0009765625
- qkv_m: float32 [768, 3, 768], P('batch', None, 'mp'), may hold values from -0.0009765625 to 0.0009765625
- out_m: float32 [768, 768], P('mp', 'batch'), may hold values from -0.0009765625 to 0.0009765625
- gate_up_m: float32 [768, 2, 3072], P('batch', None, 'mp'), may hold values from -0.0009765625 to 0.0009765625
- down_m: float32 [3072, 768], P('mp', 'batch'), may hold values from -0.0009765625 to 0.0009765625
- gains_m: float32 [2, 768], P(None, 'batch'), may hold values from -0.0009765625 to 0.0009765625
- table_v: float32 [30528, 768], P('batch'), may hold values from 3.040972e-08 to 1.2163888e-07
- qkv_v: float32 [768, 3, 768], P('batch', None, 'mp'), may hold values from 3.040972e-08 to 1.2163888e-07
- out_v: float32 [768, 768], P('mp', 'batch'), may hold values from 3.040972e-08 to 1.2163888e-07
- gate_up_v: float32 [768, 2, 3072], P('batch', None, 'mp'), may hold values from 3.040972e-08 to 1.2163888e-07
- down_v: float32 [3072, 768], P('mp', 'batch'), may hold values from 3.040972e-08 to 1.2163888e-07
- gains_v: float32 [2, 768], P(None, 'batch'), may hold values from 3.040972e-08 to 1.2163888e-07
Outputs:
- loss: float32 [1], replicated
- grad_norm: float32 [1], replicated
- new_table: float32 [30528, 768], P('batch')
- new_qkv_weight: float32 [768, 3, 768], P('batch', None, 'mp')
- new_out_weight: float32 [768, 768], P('mp', 'batch')
- new_gate_up_weight: float32 [768, 2, 3072], P('batch', None, 'mp')
- new_down_weight: float32 [3072, 768], P('mp', 'batch')
- new_gains: float32 [2, 768], P(None, 'batch')
- clipped_table_grad: float32 [30528, 768], P('batch')
- new_qkv_m: float32 [768, 3, 768], P('batch', None, 'mp')
- new_out_m: float32 [768, 768], P('mp', 'batch')
- new_gate_up_m: float32 [768, 2, 3072], P('batch', None, 'mp')
- new_down_m: float32 [3072, 768], P('mp', 'batch')
- new_gains_m: float32 [2, 768], P(None, 'batch')
- new_table_v: float32 [30528, 768], P('batch')
- new_qkv_v: float32 [768, 3, 768], P('batch', None, 'mp')
- new_out_v: float32 [768, 768], P('mp', 'batch')
- new_gate_up_v: float32 [768, 2, 3072], P('batch', None, 'mp')
- new_down_v: float32 [3072, 768], P('mp', 'batch')
- new_gains_v: float32 [2, 768], P(None, 'batch')
Inputs may be any that keep to these rules, and one draw needn't show every extreme that they name: `segment_ids`: in each row the ids never fall, every id 0 to 8 appears, id 8 marks padding, each segment has 1 to 1024 tokens and one has exactly 1024. A permutation: token t's embedding is table row row_of[t]. The first query_count queries count.
All inputs are finite; a program needn't handle non-finite values.
Results may differ from a plain program's by a relative error of at most 0.0075.
The roundings to bfloat16 on the way count: a program that leaves them out, or rounds other values in their place, can miss the bound.
Values may be sent and summed in bfloat16 or wider, within the bound.
A program may use at most 320 MiB of HBM per device.

v0:
```python
from functools import partial
import jax
import jax.numpy as jnp
from jax import lax
from jax.sharding import PartitionSpec as P

D = 768
HEAD_DIM = 64
SEGS = 8
peak_affinity = lax.Precision.HIGHEST
sharpness_divisor = 0.05
clip_limit = 1.0
step_number = 3.0
rates = (0.3, 0.02, 0.02, 0.02, 0.02, 0.3)
negative = -1e30


def positions(segment_row, segment_count):
    labels = jnp.arange(segment_count + 1, dtype=jnp.int32)
    member = (segment_row[:, None] == labels[None, :]).astype(jnp.int32)
    counts = jnp.sum(member, 0)
    starts = jnp.cumsum(counts) - counts
    first_index = jnp.sum(member * starts[None, :], 1)
    return (jnp.arange(segment_row.shape[0], dtype=jnp.int32) - first_index).astype(jnp.float32)


def rotate(values, places):
    half_dim = values.shape[-1] // 2
    freqs = jnp.power(1000.0, -2.0 * jnp.arange(half_dim, dtype=jnp.float32) / values.shape[-1])
    angles = places[:, None] * freqs[None, :]
    cosine = jnp.cos(angles)[:, None, :]
    sine = jnp.sin(angles)[:, None, :]
    former = values[..., :half_dim]
    latter = values[..., half_dim:]
    return jnp.concatenate([former * cosine - latter * sine, latter * cosine + former * sine], -1)


def layer_norm(values, gain):
    centred = values - jnp.mean(values, -1, keepdims=True)
    spread = jnp.mean(centred * centred, -1, keepdims=True)
    return centred * lax.rsqrt(spread + 1e-05) * gain


def swiglu(gate_up):
    return jax.nn.silu(gate_up[:, 0]) * gate_up[:, 1]


def contract(left, right, left_dim, right_dim):
    return lax.dot_general(
        left, right, (((left_dim,), (right_dim,)), ((), ())), preferred_element_type=jnp.float32
    )


def pool_rows(hidden, segment_ids):
    rows_dev, length = segment_ids.shape
    labels = jnp.arange(SEGS, dtype=jnp.int32)
    member = (segment_ids[:, None, :] == labels[None, :, None]).astype(jnp.float32)
    sums = jnp.einsum(
        "rsl,rld->rsd", member, hidden.reshape(rows_dev, length, -1), precision=peak_affinity
    )
    pooled = (sums / jnp.sum(member, -1, keepdims=True)).reshape(rows_dev * SEGS, -1)
    return pooled * lax.rsqrt(jnp.sum(pooled * pooled, -1, keepdims=True) + 1e-06)


def block_scores(query_block, key_row, segment_block, segment_row):
    scores = jnp.einsum(
        "qhd,khd->hqk", query_block, key_row, preferred_element_type=jnp.float32
    ) * HEAD_DIM ** (-0.5)
    same = segment_block[:, None] == segment_row[None, :]
    return jnp.where(same[None], scores, negative)


def attend(query, keys, values, segment_ids, width):
    rows_dev, length = segment_ids.shape
    per_row = length // width
    flat_segments = segment_ids.reshape(-1)

    def one_block(block):
        row_index = block // per_row
        query_block = lax.dynamic_slice_in_dim(query, block * width, width, 0)
        segment_block = lax.dynamic_slice_in_dim(flat_segments, block * width, width, 0)
        scores = block_scores(query_block, keys[row_index], segment_block, segment_ids[row_index])
        peak_score = jnp.max(scores, -1, keepdims=True)
        weights = jnp.exp(scores - peak_score)
        totals = jnp.sum(weights, -1, keepdims=True)
        probs = (weights / totals).astype(jnp.bfloat16)
        output = jnp.einsum(
            "hqk,khd->qhd", probs, values[row_index], preferred_element_type=jnp.float32
        )
        return (output, (peak_score + jnp.log(totals))[..., 0])

    outputs, log_totals = lax.map(one_block, jnp.arange(rows_dev * per_row, dtype=jnp.int32))
    return (outputs.reshape((rows_dev * length,) + outputs.shape[2:]), log_totals)


def attend_back(query, keys, values, segment_ids, log_totals, grad_out, width):
    rows_dev, length = segment_ids.shape
    per_row = length // width
    flat_segments = segment_ids.reshape(-1)
    factor = HEAD_DIM ** (-0.5)

    def one_block(carry, block):
        grad_keys, grad_values = carry
        row_index = block // per_row
        query_block = lax.dynamic_slice_in_dim(query, block * width, width, 0)
        segment_block = lax.dynamic_slice_in_dim(flat_segments, block * width, width, 0)
        grad_block = lax.dynamic_slice_in_dim(grad_out, block * width, width, 0)
        scores = block_scores(query_block, keys[row_index], segment_block, segment_ids[row_index])
        probs = jnp.exp(scores - log_totals[block][..., None])
        grad_probs = jnp.einsum(
            "qhd,khd->hqk", grad_block, values[row_index], preferred_element_type=jnp.float32
        )
        inner = jnp.sum(probs * grad_probs, -1, keepdims=True)
        grad_scores = (probs * (grad_probs - inner)).astype(jnp.bfloat16)
        grad_query = (
            jnp.einsum(
                "hqk,khd->qhd", grad_scores, keys[row_index], preferred_element_type=jnp.float32
            )
            * factor
        )
        key_term = (
            jnp.einsum("hqk,qhd->khd", grad_scores, query_block, preferred_element_type=jnp.float32)
            * factor
        )
        value_term = jnp.einsum(
            "hqk,qhd->khd",
            probs.astype(jnp.bfloat16),
            grad_block,
            preferred_element_type=jnp.float32,
        )
        return (
            (grad_keys.at[row_index].add(key_term), grad_values.at[row_index].add(value_term)),
            grad_query,
        )

    zeros = jnp.zeros(keys.shape, jnp.float32)
    (grad_keys, grad_values), grad_query = lax.scan(
        one_block, (zeros, zeros), jnp.arange(rows_dev * per_row, dtype=jnp.int32)
    )
    return (grad_query.reshape((rows_dev * length,) + grad_query.shape[2:]), grad_keys, grad_values)


def adam_update(weight, grad, first, second, rate):
    first = 0.5 * first + 0.5 * grad
    second = 0.5 * second + 0.5 * grad * grad
    correction = 1.0 - 0.5**step_number
    weight = weight - rate * (
        first / correction / (jnp.sqrt(second / correction) + 1e-08) + 0.01 * weight
    )
    return (weight, first, second)


def local(
    token_ids,
    segment_ids,
    row_of,
    query_count,
    table,
    qkv_weight,
    out_weight,
    gate_up_weight,
    down_weight,
    gains,
    table_m,
    qkv_m,
    out_m,
    gate_up_m,
    down_m,
    gains_m,
    table_v,
    qkv_v,
    out_v,
    gate_up_v,
    down_v,
    gains_v,
):
    local_width = table.shape[1] // lax.axis_size("mp")
    column = lax.axis_index("mp") * local_width
    table_cols = lax.dynamic_slice_in_dim(table, column, local_width, 1)
    low_table, w_qkv, w_out, w_gu, w_down, gain_low = (
        lax.all_gather(table_cols.astype(jnp.bfloat16), "batch", axis=0, tiled=True),
        lax.all_gather(qkv_weight.astype(jnp.bfloat16), "batch", axis=0, tiled=True),
        lax.all_gather(out_weight.astype(jnp.bfloat16), "batch", axis=1, tiled=True),
        lax.all_gather(gate_up_weight.astype(jnp.bfloat16), "batch", axis=0, tiled=True),
        lax.all_gather(down_weight.astype(jnp.bfloat16), "batch", axis=1, tiled=True),
        lax.all_gather(gains.astype(jnp.bfloat16), "batch", axis=1, tiled=True),
    )
    gain = gain_low.astype(jnp.float32)
    rows_dev, length = token_ids.shape
    tokens = rows_dev * length
    width = min(512, length)
    heads_local = w_qkv.shape[2] // HEAD_DIM
    ff_local = w_gu.shape[2]
    table_rows = row_of[token_ids.reshape(-1)]
    x_zero = lax.all_gather(low_table[table_rows], "mp", axis=1, tiled=True)
    places = jax.vmap(partial(positions, segment_count=SEGS))(segment_ids).reshape(-1)
    qkv = jnp.dot(x_zero, w_qkv.reshape(D, -1), preferred_element_type=jnp.float32).reshape(
        tokens, 3, heads_local, HEAD_DIM
    )
    query = rotate(qkv[:, 0], places).astype(jnp.bfloat16)
    keys = (
        rotate(qkv[:, 1], places)
        .astype(jnp.bfloat16)
        .reshape(rows_dev, length, heads_local, HEAD_DIM)
    )
    values = qkv[:, 2].astype(jnp.bfloat16).reshape(rows_dev, length, heads_local, HEAD_DIM)
    attended, log_totals = attend(query, keys, values, segment_ids, width)
    attended_low = attended.reshape(tokens, -1).astype(jnp.bfloat16)
    attn_term = jnp.dot(attended_low, w_out, preferred_element_type=jnp.float32)
    attn = lax.psum(attn_term, "mp")
    hidden_one, first_back = jax.vjp(layer_norm, x_zero.astype(jnp.float32) + attn, gain[0])
    hidden_low = hidden_one.astype(jnp.bfloat16)
    gate_up = jnp.dot(hidden_low, w_gu.reshape(D, -1), preferred_element_type=jnp.float32).reshape(
        tokens, 2, ff_local
    )
    active, swiglu_back = jax.vjp(swiglu, gate_up)
    active_low = active.astype(jnp.bfloat16)
    mlp = lax.psum(jnp.dot(active_low, w_down, preferred_element_type=jnp.float32), "mp")
    hidden_two, second_back = jax.vjp(layer_norm, hidden_one + mlp, gain[1])
    embed, pool_back = jax.vjp(lambda hidden: pool_rows(hidden, segment_ids), hidden_two)
    batch_index = lax.axis_index("batch")
    half_count = lax.axis_size("batch") // 2
    texts = embed.shape[0]
    queries_all = half_count * texts
    everyone = lax.all_gather(embed, "batch", axis=0, tiled=True)
    question_vectors = everyone[:queries_all]
    passage_vectors = everyone[queries_all:]
    limit = query_count[0].astype(jnp.float32)
    labels = jnp.arange(queries_all, dtype=jnp.int32)
    weight_rows = (labels < query_count[0]).astype(jnp.float32) / limit
    affinity_scores = (
        jnp.dot(question_vectors, passage_vectors.T, precision=peak_affinity) / sharpness_divisor
    )
    target = (labels[:, None] == labels[None, :]).astype(jnp.float32)
    loss_value = jnp.sum(
        weight_rows
        * (jax.nn.logsumexp(affinity_scores, -1) - jnp.sum(affinity_scores * target, -1))
    )
    affinity_derivative = (jax.nn.softmax(affinity_scores, -1) - target) * weight_rows[:, None]
    grad_all = jnp.concatenate(
        [
            jnp.dot(affinity_derivative, passage_vectors, precision=peak_affinity)
            / sharpness_divisor,
            jnp.dot(affinity_derivative.T, question_vectors, precision=peak_affinity)
            / sharpness_divisor,
        ],
        0,
    )
    grad_embed = lax.dynamic_slice_in_dim(grad_all, batch_index * texts, texts, 0)
    (grad_two,) = pool_back(grad_embed)
    grad_second, grad_gain_two = second_back(grad_two)
    grad_mlp_low = grad_second.astype(jnp.bfloat16)
    grad_active = contract(grad_mlp_low, w_down, 1, 1)
    grad_down = contract(active_low, grad_mlp_low, 0, 0)
    (grad_gate_up,) = swiglu_back(grad_active)
    grad_gu_low = grad_gate_up.reshape(tokens, -1).astype(jnp.bfloat16)
    back_term = contract(grad_gu_low, w_gu.reshape(D, -1), 1, 1)
    grad_one = grad_second + lax.psum(back_term, "mp")
    grad_first, grad_gain_one = first_back(grad_one)
    grad_gu = contract(hidden_low, grad_gu_low, 0, 0)
    grad_attn_low = grad_first.astype(jnp.bfloat16)
    grad_attended = contract(grad_attn_low, w_out, 1, 1).astype(jnp.bfloat16)
    grad_out = contract(attended_low, grad_attn_low, 0, 0)
    grad_query, grad_keys, grad_values = attend_back(
        query,
        keys,
        values,
        segment_ids,
        log_totals,
        grad_attended.reshape(tokens, heads_local, HEAD_DIM),
        width,
    )
    _, rotate_back = jax.vjp(lambda inputs: rotate(inputs, places), qkv[:, 0])
    (grad_query_raw,) = rotate_back(grad_query)
    (grad_key_raw,) = rotate_back(grad_keys.reshape(tokens, heads_local, HEAD_DIM))
    grad_qkv_low = (
        jnp.stack(
            [grad_query_raw, grad_key_raw, grad_values.reshape(tokens, heads_local, HEAD_DIM)], 1
        )
        .reshape(tokens, -1)
        .astype(jnp.bfloat16)
    )
    grad_zero = grad_first + lax.psum(contract(grad_qkv_low, w_qkv.reshape(D, -1), 1, 1), "mp")
    grad_qkv = contract(x_zero, grad_qkv_low, 0, 0)
    grad_table = (
        jnp.zeros((low_table.shape[0], local_width), jnp.float32)
        .at[table_rows]
        .add(lax.dynamic_slice_in_dim(grad_zero, column, local_width, 1))
    )
    grad_gains = jnp.stack([grad_gain_one, grad_gain_two], 0)
    reduced = (
        lax.psum_scatter(grad_table, "batch", scatter_dimension=0, tiled=True),
        lax.psum_scatter(grad_qkv.reshape(D, 3, -1), "batch", scatter_dimension=0, tiled=True),
        lax.psum_scatter(grad_out, "batch", scatter_dimension=1, tiled=True),
        lax.psum_scatter(grad_gu.reshape(D, 2, -1), "batch", scatter_dimension=0, tiled=True),
        lax.psum_scatter(grad_down, "batch", scatter_dimension=1, tiled=True),
        lax.psum_scatter(grad_gains, "batch", scatter_dimension=1, tiled=True),
    )
    squares = sum((jnp.sum(part * part) for part in reduced[:5])) + jnp.sum(
        reduced[5] * reduced[5]
    ) / lax.axis_size("mp")
    table_full = lax.all_gather(reduced[0], "mp", axis=1, tiled=True)
    total_squares = lax.psum(squares, ("batch", "mp"))
    grad_norm = jnp.sqrt(total_squares)
    scale = clip_limit / jnp.maximum(grad_norm, clip_limit)
    olds = (table, qkv_weight, out_weight, gate_up_weight, down_weight, gains)
    grads_all = (table_full,) + tuple(reduced[1:])
    firsts = (table_m, qkv_m, out_m, gate_up_m, down_m, gains_m)
    seconds = (table_v, qkv_v, out_v, gate_up_v, down_v, gains_v)
    updated = [
        adam_update(weight_old, grad_part * scale, first_old, second_old, rate)
        for weight_old, grad_part, first_old, second_old, rate in zip(
            olds, grads_all, firsts, seconds, rates
        )
    ]
    clipped_table = table_full * scale
    loss = loss_value.reshape(1)
    return (
        loss,
        grad_norm.reshape(1),
        updated[0][0],
        updated[1][0],
        updated[2][0],
        updated[3][0],
        updated[4][0],
        updated[5][0],
        clipped_table,
        updated[1][1],
        updated[2][1],
        updated[3][1],
        updated[4][1],
        updated[5][1],
        updated[0][2],
        updated[1][2],
        updated[2][2],
        updated[3][2],
        updated[4][2],
        updated[5][2],
    )


def solution(mesh):
    placed = (
        P("batch", None),
        P("batch", None),
        P(),
        P(),
        P("batch", None),
        P("batch", None, "mp"),
        P("mp", "batch"),
        P("batch", None, "mp"),
        P("mp", "batch"),
        P(None, "batch"),
        P("batch", None),
        P("batch", None, "mp"),
        P("mp", "batch"),
        P("batch", None, "mp"),
        P("mp", "batch"),
        P(None, "batch"),
        P("batch", None),
        P("batch", None, "mp"),
        P("mp", "batch"),
        P("batch", None, "mp"),
        P("mp", "batch"),
        P(None, "batch"),
    )
    return jax.shard_map(
        local,
        mesh=mesh,
        in_specs=placed,
        out_specs=(
            P(),
            P(),
            P("batch", None),
            P("batch", None, "mp"),
            P("mp", "batch"),
            P("batch", None, "mp"),
            P("mp", "batch"),
            P(None, "batch"),
            P("batch", None),
            P("batch", None, "mp"),
            P("mp", "batch"),
            P("batch", None, "mp"),
            P("mp", "batch"),
            P(None, "batch"),
            P("batch", None),
            P("batch", None, "mp"),
            P("mp", "batch"),
            P("batch", None, "mp"),
            P("mp", "batch"),
            P(None, "batch"),
        ),
        check_vma=False,
    )
```

profile of v0, /device:TPU:0, one launch (start us, length us, event | category | flops | bytes accessed | tf_op | source)
XLA Modules:
  0.0 1895.6 jit_solution(3074774490312549609)
XLA Ops:
  7.3 12.4 copy.141
  31.4 63.1 %all-gather.17.cloned.1.call-done = bf16[8,3816,192]{1,2,0:T(8,128)(2,1)} async-done(((bf16[1,3816,192]{1,2,0:T(8,128)(2,1)}), bf16[8,3816,192]{1,2,0:T(8,128)(2,1)}) %all-gather.17.cloned.1.call-update) | async-done | bytes 11722768 | tf_op jit(solution)/shard_map/all_gather | solution.py:181
  94.5 18.1 copy.142
  112.6 11.2 gather_fusion.1
  126.6 13.2 all_gather.29
  151.9 23.6 %all-gather.15.cloned.1.call-done = bf16[1536,768]{0,1:T(8,128)(2,1)} async-done(((bf16[1536,192]{0,1:T(8,128)(2,1)}), bf16[1536,768]{0,1:T(8,128)(2,1)}) %all-gather.15.cloned.1.call-update) | async-done | bytes 2359312 | tf_op jit(solution)/shard_map/all_gather | solution.py:195
  179.8 33.9 %while.31 = (s32[]{:T(128)}, bf16[3,512,3,64]{1,3,2,0:T(8,128)(2,1)}, f32[3,3,512]{2,1,0:T(4,128)S(1)}, s32[3]{0:T(128)S(1)}, s32[1536]{0:T(1024)S(1)}, /*index=...) while((s32[]{:T(128)}, ...), condition=%wide.region_6.7_spmd, body=%wide.region_3.6_spmd.sunk | while | flops 633076224 | bytes 38029568 | solution.py:92
  232.6 156.8 %all-reduce.11.cloned.1.call-done = f32[1536,768]{0,1:T(8,128)} async-done(((f32[1536,768]{0,1:T(8,128)}), f32[1536,768]{0,1:T(8,128)}) %all-reduce.11.cloned.1.call-update) | async-done | bytes 4718608 | tf_op jit(solution)/shard_map/psum | solution.py:210
  421.9 171.2 %all-reduce.13.cloned.1.call-done = f32[1536,768]{0,1:T(8,128)} async-done(((f32[1536,768]{0,1:T(8,128)}), f32[1536,768]{0,1:T(8,128)}) %all-reduce.13.cloned.1.call-update) | async-done | bytes 4718608 | tf_op jit(solution)/shard_map/psum | solution.py:218
  601.2 9.5 all_gather.34
  633.7 169.7 %all-reduce.15.cloned.1.call-done = f32[1536,768]{0,1:T(8,128)} async-done(((f32[1536,768]{0,1:T(8,128)}), f32[1536,768]{0,1:T(8,128)}) %all-reduce.15.cloned.1.call-update) | async-done | bytes 4718608 | tf_op jit(solution)/shard_map/psum | solution.py:258
  821.4 161.7 %while.32 = (s32[]{:T(128)}, f32[1,1536,3,64]{1,3,2,0:T(8,128)}, f32[1,1536,3,64]{1,3,2,0:T(8,128)S(1)}, f32[3,512,3,64]{1,0,3,2:T(4,128)}, s32[3]{0:T(128)S(1)}...) while((s32[]{:T(128)}, f32[1,1536,3,64]{1,3,2,0:T(8,128)}, ...), condition=%wide.region_29.30_spmd.clone, body=%wide.region_26.29_spmd.clone.sunk | while | flops 1534130688 | bytes 86367704 | solution.py:137
  839.3 9.4 multiply_convert_fusion.4
  893.0 9.4 multiply_convert_fusion.4
  993.0 171.1 %all-reduce.17.cloned.1.call-done = f32[1536,768]{0,1:T(8,128)} async-done(((f32[1536,768]{0,1:T(8,128)}), f32[1536,768]{0,1:T(8,128)}) %all-reduce.17.cloned.1.call-update) | async-done | bytes 4718608 | tf_op jit(solution)/shard_map/psum | solution.py:283
  1166.3 21.2 %scatter_custom_fusion = f32[30528,192]{1,0:T(8,128)} fusion(s32[1536]{0:T(1024)} %copy-done.49, f32[1536,192]{1,0:T(8,128)S(1)} %copy.157, f32[]{:T(128)} %constant.228.clone.1), kind=kCustom, calls=%fused_computation.51 | custom fusion | flops 294912 | bytes 23446016 | tf_op jit(solution)/shard_map/scatter-add | solution.py:288
  1201.7 15.3 fusion.50
  1224.7 151.4 %reduce-scatter.11.cloned.1.call-done = f32[3816,192]{1,0:T(8,128)} async-done(((f32[30528,192]{1,0:T(8,128)}), f32[3816,192]{1,0:T(8,128)}) %reduce-scatter.11.cloned.1.call-update) | async-done | bytes 2930704 | tf_op jit(solution)/shard_map/reduce_scatter | solution.py:292
  1381.2 12.6 copy.160
  1393.8 28.0 %reduce-scatter.17.cloned.1.call-done = f32[768,96]{0,1:T(8,128)} async-done(((f32[768,768]{0,1:T(8,128)}), f32[768,96]{0,1:T(8,128)}) %reduce-scatter.17.cloned.1.call-update) | async-done | bytes 294928 | tf_op jit(solution)/shard_map/reduce_scatter | solution.py:296
  1423.5 36.1 %reduce-scatter.21.cloned.1.call-done = f32[96,2]{1,0:T(8,128)} async-done(((f32[768,2]{1,0:T(8,128)}), f32[96,2]{1,0:T(8,128)}) %reduce-scatter.21.cloned.1.call-update) | async-done | bytes 784
  1461.8 36.2 %reduce-scatter.19.cloned.1.call-done = f32[96,192]{1,0:T(8,128)} async-done(((f32[768,192]{1,0:T(8,128)}), f32[96,192]{1,0:T(8,128)}) %reduce-scatter.19.cloned.1.call-update) | async-done | bytes 73744
  1499.6 56.7 %reduce-scatter.15.cloned.1.call-done = f32[96,2,768]{2,0,1:T(8,128)} async-done(((f32[768,2,768]{2,0,1:T(8,128)}), f32[96,2,768]{2,0,1:T(8,128)}) %reduce-scatter.15.cloned.1.call-update) | async-done | bytes 589840 | tf_op jit(solution)/shard_map/reduce_scatter | solution.py:295
  1558.1 44.5 %reduce-scatter.13.cloned.1.call-done = f32[96,3,192]{2,0,1:T(8,128)} async-done(((f32[768,3,192]{2,0,1:T(8,128)}), f32[96,3,192]{2,0,1:T(8,128)}) %reduce-scatter.13.cloned.1.call-update) | async-done | bytes 221200 | tf_op jit(solution)/shard_map/reduce_scatter | solution.py:293
  1611.3 13.3 copy.158
  1624.7 53.5 %psum.39 = f32[]{:T(128)} all-reduce(f32[]{:T(128)S(6)} %add.324), channel_id=1, replica_groups=mesh['batch'=8,'mp'=4] {'batch','mp'}, use_global_device_ids=true, to_apply=%region_46.47 | all-reduce | flops 1 | bytes 8 | tf_op jit(solution)/shard_map/psum | solution.py:303
  1687.7 123.4 %all-gather.13.cloned.1.call-done = f32[3816,768]{0,1:T(8,128)} async-done(((f32[3816,192]{0,1:T(8,128)}), f32[3816,768]{0,1:T(8,128)}) %all-gather.13.cloned.1.call-update) | async-done | bytes 11722768 | tf_op jit(solution)/shard_map/all_gather | solution.py:302
  1811.0 17.3 fusion.46
  1828.4 12.3 copy.169
  1840.7 22.2 %fusion.45 = f32[3816,768]{0,1:T(8,128)} fusion(f32[3816,768]{0,1:T(8,128)} %copy.141, f32[3816,768]{0,1:T(8,128)} %get-tuple-element.440, f32[3816,768]{0,1:T(8,128)} %copy.158, f32[3816,768]{0,1:T(8,128)} %copy.160), kind=kLoop, calls=%fused_computation.57 | loop fusion | flops 41029632 | bytes 58613760 | tf_op jit(solution)/shard_map/sub | solution.py:147
  1862.9 12.3 copy.167
  1875.3 12.4 copy.171
  (347 shorter events, 350.5 us)
Async XLA Ops:
  7.2 87.3 %all-gather.17.cloned.1.call-start = ((), (), s32[]{:S(2)}) async-start(), calls=%async_computation.18 | async-start | bytes 13271040 | tf_op jit(solution)/shard_map/all_gather | solution.py:181
  22.8 152.7 %all-gather.15.cloned.1.call-start = ((), (), s32[]{:S(2)}) async-start(), calls=%async_computation.17 | async-start | bytes 2949120 | tf_op jit(solution)/shard_map/all_gather | solution.py:195
  31.4 81.2 %copy-start.49 = (s32[1536]{0:T(1024)}, s32[1536]{0:T(1024)S(1)}, u32[]{:S(2)}) copy-start(s32[1536]{0:T(1024)S(1)} %fusion.104) | copy-start | bytes 18436
  124.8 103.5 %all-gather.9.cloned.1.call-start = ((), (), s32[]{:S(2)}) async-start(), calls=%async_computation.7 | async-start | bytes 2654208 | tf_op jit(solution)/shard_map/all_gather | solution.py:184
  125.7 263.7 %all-reduce.11.cloned.1.call-start = ((), (), s32[]{:S(2)}) async-start(), calls=%async_computation.6 | async-start | bytes 9437184 | tf_op jit(solution)/shard_map/psum | solution.py:210
  151.1 64.4 %copy-start.10 = (bf16[192,768]{0,1:T(8,128)(2,1)}, bf16[192,768]{0,1:T(8,128)(2,1)S(1)}, u32[]{:S(2)}) copy-start(bf16[192,768]{0,1:T(8,128)(2,1)S(1)} %all_gather.30) | copy-start | bytes 884740
  218.5 196.3 %all-gather.11.cloned.1.call-start = ((), (), s32[]{:S(2)}) async-start(), calls=%async_computation.8 | async-start | bytes 1327104 | tf_op jit(solution)/shard_map/all_gather | solution.py:185
  219.2 373.9 %all-reduce.13.cloned.1.call-start = ((), (), s32[]{:S(2)}) async-start(), calls=%async_computation.9 | async-start | bytes 9437184 | tf_op jit(solution)/shard_map/psum | solution.py:218
  228.3 585.8 %copy-start.45 = (f32[768]{0:T(1024)}, f32[768]{0:T(1024)S(1)}, u32[]{:S(2)}) copy-start(f32[768]{0:T(1024)S(1)} %get-tuple-element.396) | copy-start | bytes 9220
  393.4 420.7 %copy-start.41 = (f32[1536]{0:T(1024)}, f32[1536]{0:T(1024)S(1)}, u32[]{:S(2)}) copy-start(f32[1536]{0:T(1024)S(1)} %broadcast_multiply_fusion.3) | copy-start | bytes 18436
  393.9 420.1 %copy-start.43 = (f32[1536]{0:T(1024)}, f32[1536]{0:T(1024)S(1)}, u32[]{:S(2)}) copy-start(f32[1536]{0:T(1024)S(1)} %fusion.101) | copy-start | bytes 18436
  421.0 382.4 %all-reduce.15.cloned.1.call-start = ((), (), s32[]{:S(2)}) async-start(), calls=%async_computation.10 | async-start | bytes 9437184 | tf_op jit(solution)/shard_map/psum | solution.py:258
  617.5 185.9 %copy-start.47 = (f32[1536]{0:T(1024)}, f32[1536]{0:T(1024)S(1)}, u32[]{:S(2)}) copy-start(f32[1536]{0:T(1024)S(1)} %negate_multiply_fusion.1) | copy-start | bytes 18436
  633.2 530.8 %all-reduce.17.cloned.1.call-start = ((), (), s32[]{:S(2)}) async-start(), calls=%async_computation.11 | async-start | bytes 9437184 | tf_op jit(solution)/shard_map/psum | solution.py:283
  821.4 163.9 %copy-start.20 = (f32[1536,32]{0,1:T(8,128)S(1)}, f32[1536,32]{0,1:T(8,128)}, u32[]{:S(2)}) copy-start(f32[1536,32]{0,1:T(8,128)} %copy-done.19) | copy-start | bytes 589828
  992.9 383.2 %reduce-scatter.11.cloned.1.call-start = ((), (), s32[]{:S(2)}) async-start(), calls=%async_computation.12 | async-start | bytes 35168256 | tf_op jit(solution)/shard_map/reduce_scatter | solution.py:292
  1187.5 234.4 %reduce-scatter.17.cloned.1.call-start = ((), (), s32[]{:S(2)}) async-start(), calls=%async_computation.15 | async-start | bytes 2654208 | tf_op jit(solution)/shard_map/reduce_scatter | solution.py:296
  1194.9 264.7 %reduce-scatter.21.cloned.1.call-start = ((), (), s32[]{:S(2)}) async-start(), calls=%async_computation.20 | async-start | bytes 442368
  1196.0 302.0 %reduce-scatter.19.cloned.1.call-start = ((), (), s32[]{:S(2)}) async-start(), calls=%async_computation.19 | async-start | bytes 884736
  1201.7 354.7 %reduce-scatter.15.cloned.1.call-start = ((), (), s32[]{:S(2)}) async-start(), calls=%async_computation.14 | async-start | bytes 5308416 | tf_op jit(solution)/shard_map/reduce_scatter | solution.py:295
  1217.1 385.6 %reduce-scatter.13.cloned.1.call-start = ((), (), s32[]{:S(2)}) async-start(), calls=%async_computation.13 | async-start | bytes 2654208 | tf_op jit(solution)/shard_map/reduce_scatter | solution.py:293
  1224.7 586.4 %all-gather.13.cloned.1.call-start = ((), (), s32[]{:S(2)}) async-start(), calls=%async_computation.16 | async-start | bytes 14745600 | tf_op jit(solution)/shard_map/all_gather | solution.py:302
  1611.3 67.6 %copy-start.13 = (f32[96,2,768]{2,1,0:T(2,128)S(1)}, f32[96,2,768]{2,1,0:T(2,128)}, u32[]{:S(2)}) copy-start(f32[96,2,768]{2,1,0:T(2,128)} %param.37) | copy-start | bytes 1769476
  1611.3 67.6 %copy-start.14 = (f32[96,2,768]{2,0,1:T(8,128)S(1)}, f32[96,2,768]{2,0,1:T(8,128)}, u32[]{:S(2)}) copy-start(f32[96,2,768]{2,0,1:T(8,128)} %reduce-scatter.15.cloned.1.call-done) | copy-start | bytes 1769476
  1611.3 67.6 %copy-start.31 = (f32[96,2,768]{2,1,0:T(2,128)S(1)}, f32[96,2,768]{2,1,0:T(2,128)}, u32[]{:S(2)}) copy-start(f32[96,2,768]{2,1,0:T(2,128)} %param.43) | copy-start | bytes 1769476
  1611.3 67.6 %copy-start.32 = (f32[96,2,768]{2,1,0:T(2,128)S(1)}, f32[96,2,768]{2,1,0:T(2,128)}, u32[]{:S(2)}) copy-start(f32[96,2,768]{2,1,0:T(2,128)} %param.49) | copy-start | bytes 1769476
  1624.6 58.6 %copy-start.55 = (f32[2,96]{1,0:T(2,128)S(1)}, f32[2,96]{1,0:T(2,128)}, u32[]{:S(2)}) copy-start(f32[2,96]{1,0:T(2,128)} %param.45) | copy-start | bytes 2308
  1624.6 58.6 %copy-start.56 = (f32[2,96]{1,0:T(2,128)S(1)}, f32[2,96]{1,0:T(2,128)}, u32[]{:S(2)}) copy-start(f32[2,96]{1,0:T(2,128)} %param.51) | copy-start | bytes 2308
  1624.6 59.2 %copy-start.36 = (f32[192,96]{1,0:T(8,128)S(1)}, f32[192,96]{1,0:T(8,128)}, u32[]{:S(2)}) copy-start(f32[192,96]{1,0:T(8,128)} %param.36) | copy-start | bytes 221188
  1624.6 60.9 %copy-start.24 = (f32[768,96]{0,1:T(8,128)S(1)}, f32[768,96]{0,1:T(8,128)}, u32[]{:S(2)}) copy-start(f32[768,96]{0,1:T(8,128)} %param.38) | copy-start | bytes 884740
  1624.6 60.9 %copy-start.27 = (f32[768,96]{0,1:T(8,128)S(1)}, f32[768,96]{0,1:T(8,128)}, u32[]{:S(2)}) copy-start(f32[768,96]{0,1:T(8,128)} %reduce-scatter.17.cloned.1.call-done) | copy-start | bytes 884740
  1624.6 60.9 %copy-start.37 = (f32[768,96]{0,1:T(8,128)S(1)}, f32[768,96]{0,1:T(8,128)}, u32[]{:S(2)}) copy-start(f32[768,96]{0,1:T(8,128)} %param.44) | copy-start | bytes 884740
  (53 other events, 413.0 us)
Sparse Core Ops, SparseCore 0:
  22.9 71.4 all-gather.16
  125.0 50.4 all-gather.14
  178.0 27.8 all-gather.8
  218.6 170.7 all-reduce.10
  391.7 23.0 all-gather.10
  421.1 171.9 all-reduce.12
  633.3 170.0 all-reduce.14
  993.0 170.9 all-reduce.16
  1187.6 188.4 reduce-scatter.10
  1379.3 42.5 reduce-scatter.16
  1425.8 33.7 reduce-scatter.20
  1463.0 34.9 reduce-scatter.18
  1502.4 53.8 reduce-scatter.14
  1560.1 42.5 reduce-scatter.12
  1604.7 206.2 all-gather.12
where the time goes:
time: 1900 us
  waiting for transfers between devices  1240 us (65%)
  local copies, waits for them, and re-layouts  191 us (10%)
  matrix products  179 us (9%)
  other arithmetic  153 us (8%)
  blocking collectives  94.2 us (5%)
  between operations  21.7 us (1%)
    psum x1, waiting for transfers between devices, local(): lax.psum(jnp.dot(active_low, w_down, preferred_element_type=jnp.float32),...  171 us
    psum x1, waiting for transfers between devices, local(): lax.psum(contract(grad_qkv_low, w_qkv.reshape(D, -1), 1, 1), 'mp')  171 us
    psum x1, waiting for transfers between devices, local(): grad_one = grad_second + lax.psum(back_term, 'mp')  170 us
    psum x1, waiting for transfers between devices, local(): attn = lax.psum(attn_term, 'mp')  157 us
    reduce_scatter x1, waiting for transfers between devices, local(): lax.psum_scatter(grad_table, 'batch', scatter_dimension=0, tiled=True)  151 us
    all_gather x1, waiting for transfers between devices, local(): table_full = lax.all_gather(reduced[0], 'mp', axis=1, tiled=True)  123 us
    unnamed x132, local copies, waits for them, and re-layouts  102 us
    unnamed x17, waiting for transfers between devices  72.6 us
  transfers between devices with their start and end apart: 15, of which 14 were waited for; matrix products, arithmetic and copies ran while one was open for 8% of the time, Pallas kernels for 0%

commit v1 on v0

--- a/solution.py
+++ b/solution.py
@@ -13,6 +13,29 @@
 step_number = 3.0
 rates = (0.3, 0.02, 0.02, 0.02, 0.02, 0.3)
 negative = -1e30
+
+
+def laid_out(parts, dim):
+    parts = jnp.moveaxis(parts, 0, dim)
+    shape = parts.shape
+    return parts.reshape(*shape[:dim], shape[dim] * shape[dim + 1], *shape[dim + 2 :])
+
+
+def doubled(x, axis):
+    size, position = (lax.axis_size(axis), lax.axis_index(axis))
+    blocks, distance = (x[None], 1)
+    while distance < size:
+        partner_block = lax.ppermute(blocks, axis, [(i, i ^ distance) for i in range(size)])
+        low = position & distance == 0
+        blocks = jnp.concatenate(
+            [jnp.where(low, blocks, partner_block), jnp.where(low, partner_block, blocks)]
+        )
+        distance *= 2
+    return blocks
+
+
+def doubled_up(x, axis, dim):
+    return laid_out(doubled(x, axis), dim)
 
 
 def positions(segment_row, segment_count):
@@ -178,7 +201,7 @@
     column = lax.axis_index("mp") * local_width
     table_cols = lax.dynamic_slice_in_dim(table, column, local_width, 1)
     low_table, w_qkv, w_out, w_gu, w_down, gain_low = (
-        lax.all_gather(table_cols.astype(jnp.bfloat16), "batch", axis=0, tiled=True),
+        doubled_up(table_cols.astype(jnp.bfloat16), "batch", 0),
         lax.all_gather(qkv_weight.astype(jnp.bfloat16), "batch", axis=0, tiled=True),
         lax.all_gather(out_weight.astype(jnp.bfloat16), "batch", axis=1, tiled=True),
         lax.all_gather(gate_up_weight.astype(jnp.bfloat16), "batch", axis=0, tiled=True),

time: 1900 us -> 2050 us (1.079)
  waiting for transfers between devices: 1240 us -> 1360 us
    ppermute x0 -> x3, waiting for transfers between devices: none -> 186 us  [doubled(): lax.ppermute(blocks, axis, [(i, i ^ distance) for i in range(size)])]
    all_gather x1 -> x0, waiting for transfers between devices: 63.1 us -> none  [local(): lax.all_gather(table_cols.astype(jnp.bfloat16), 'batch', axis=0, tiled=True)]
    unnamed x132 -> x137, local copies, waits for them, and re-layouts: 102 us -> 101 us
    unnamed x17 -> x16, waiting for transfers between devices: 72.6 us -> 72.5 us
  transfers between devices with their start and end apart: 15 -> 17, of which waited for: 14 -> 16; matrix products, arithmetic and copies ran while one was open for 8% -> 7% of each run, Pallas kernels for 0% -> 0%
where the time goes in v1:
time: 2050 us; the launch traced here: 2040 us
  waiting for transfers between devices  1360 us (66%)
  local copies, waits for them, and re-layouts  191 us (9%)
  matrix products  179 us (9%)
  other arithmetic  172 us (8%)
  blocking collectives  93.9 us (5%)
  between operations  21.7 us (1%)
    ppermute x3, waiting for transfers between devices, doubled(): lax.ppermute(blocks, axis, [(i, i ^ distance) for i in range(size)])  186 us
    psum x1, waiting for transfers between devices, local(): lax.psum(jnp.dot(active_low, w_down, preferred_element_type=jnp.float32),...  171 us
    psum x1, waiting for transfers between devices, local(): lax.psum(contract(grad_qkv_low, w_qkv.reshape(D, -1), 1, 1), 'mp')  171 us
    psum x1, waiting for transfers between devices, local(): grad_one = grad_second + lax.psum(back_term, 'mp')  170 us
    psum x1, waiting for transfers between devices, local(): attn = lax.psum(attn_term, 'mp')  157 us
    reduce_scatter x1, waiting for transfers between devices, local(): lax.psum_scatter(grad_table, 'batch', scatter_dimension=0, tiled=True)  151 us
    all_gather x1, waiting for transfers between devices, local(): table_full = lax.all_gather(reduced[0], 'mp', axis=1, tiled=True)  123 us
    unnamed x137, local copies, waits for them, and re-layouts  101 us
  transfers between devices with their start and end apart: 17, of which 16 were waited for; matrix products, arithmetic and copies ran while one was open for 7% of the time, Pallas kernels for 0%

profile of v1, /device:TPU:0, one launch (start us, length us, event | category | flops | bytes accessed | tf_op | source)
XLA Modules:
  0.0 2043.4 jit_solution(2420443045732905145)
XLA Ops:
  7.3 12.4 copy.141
  31.8 64.3 %collective-permute-done.1 = bf16[2,3816,192]{1,2,0:T(8,128)(2,1)} collective-permute-done((bf16[2,3816,192]{1,2,0:T(8,128)(2,1)S(1)}, bf16[2,3816,192]{1,2,0:T(8,128)(2,1)}, u32[]{:S(2)}, u32[]{:S(2)}) %collective-permute-start.1) | collective-permute-done | bytes 2930720 | tf_op jit(solution)/shard_map/ppermute | solution.py:28
  112.8 118.7 %collective-permute-done.2 = bf16[4,3816,192]{1,2,0:T(8,128)(2,1)} collective-permute-done((bf16[4,3816,192]{1,2,0:T(8,128)(2,1)}, bf16[4,3816,192]{1,2,0:T(8,128)(2,1)}, u32[]{:S(2)}, u32[]{:S(2)}) %collective-permute-start.2) | collective-permute-done | bytes 5861408 | tf_op jit(solution)/shard_map/ppermute | solution.py:28
  241.0 18.1 copy.142
  259.1 11.2 gather_fusion.1
  272.5 13.1 all_gather.25
  298.1 25.1 %all-gather.13.cloned.1.call-done = bf16[1536,768]{0,1:T(8,128)(2,1)} async-done(((bf16[1536,192]{0,1:T(8,128)(2,1)}), bf16[1536,768]{0,1:T(8,128)(2,1)}) %all-gather.13.cloned.1.call-update) | async-done | bytes 2359312 | tf_op jit(solution)/shard_map/all_gather | solution.py:218
  327.5 33.9 %while.31 = (s32[]{:T(128)}, bf16[3,512,3,64]{1,3,2,0:T(8,128)(2,1)}, f32[3,3,512]{2,1,0:T(4,128)S(1)}, s32[3]{0:T(128)S(1)}, s32[1536]{0:T(1024)S(1)}, /*index=...) while((s32[]{:T(128)}, ...), condition=%wide.region_6.7_spmd, body=%wide.region_3.6_spmd.sunk | while | flops 633076224 | bytes 38029568 | solution.py:115
  380.3 156.8 %all-reduce.11.cloned.1.call-done = f32[1536,768]{0,1:T(8,128)} async-done(((f32[1536,768]{0,1:T(8,128)}), f32[1536,768]{0,1:T(8,128)}) %all-reduce.11.cloned.1.call-update) | async-done | bytes 4718608 | tf_op jit(solution)/shard_map/psum | solution.py:233
  569.6 171.3 %all-reduce.13.cloned.1.call-done = f32[1536,768]{0,1:T(8,128)} async-done(((f32[1536,768]{0,1:T(8,128)}), f32[1536,768]{0,1:T(8,128)}) %all-reduce.13.cloned.1.call-update) | async-done | bytes 4718608 | tf_op jit(solution)/shard_map/psum | solution.py:241
  749.0 9.5 all_gather.30
  781.4 169.7 %all-reduce.15.cloned.1.call-done = f32[1536,768]{0,1:T(8,128)} async-done(((f32[1536,768]{0,1:T(8,128)}), f32[1536,768]{0,1:T(8,128)}) %all-reduce.15.cloned.1.call-update) | async-done | bytes 4718608 | tf_op jit(solution)/shard_map/psum | solution.py:281
  969.1 161.7 %while.32 = (s32[]{:T(128)}, f32[1,1536,3,64]{1,3,2,0:T(8,128)}, f32[1,1536,3,64]{1,3,2,0:T(8,128)S(1)}, f32[3,512,3,64]{1,0,3,2:T(4,128)}, s32[3]{0:T(128)S(1)}...) while((s32[]{:T(128)}, f32[1,1536,3,64]{1,3,2,0:T(8,128)}, ...), condition=%wide.region_29.30_spmd.clone, body=%wide.region_26.29_spmd.clone.sunk | while | flops 1534130688 | bytes 86367704 | solution.py:160
  987.0 9.4 multiply_convert_fusion.4
  1140.7 171.1 %all-reduce.17.cloned.1.call-done = f32[1536,768]{0,1:T(8,128)} async-done(((f32[1536,768]{0,1:T(8,128)}), f32[1536,768]{0,1:T(8,128)}) %all-reduce.17.cloned.1.call-update) | async-done | bytes 4718608 | tf_op jit(solution)/shard_map/psum | solution.py:306
  1314.0 21.2 %scatter_custom_fusion = f32[30528,192]{1,0:T(8,128)} fusion(s32[1536]{0:T(1024)} %copy-done.52, f32[1536,192]{1,0:T(8,128)S(1)} %copy.157, f32[]{:T(128)} %constant.231.clone.1), kind=kCustom, calls=%fused_computation.51 | custom fusion | flops 294912 | bytes 23446016 | tf_op jit(solution)/shard_map/scatter-add | solution.py:311
  1349.4 15.3 fusion.50
  1372.4 151.4 %reduce-scatter.11.cloned.1.call-done = f32[3816,192]{1,0:T(8,128)} async-done(((f32[30528,192]{1,0:T(8,128)}), f32[3816,192]{1,0:T(8,128)}) %reduce-scatter.11.cloned.1.call-update) | async-done | bytes 2930704 | tf_op jit(solution)/shard_map/reduce_scatter | solution.py:315
  1528.9 12.6 copy.160
  1541.5 28.2 %reduce-scatter.17.cloned.1.call-done = f32[768,96]{0,1:T(8,128)} async-done(((f32[768,768]{0,1:T(8,128)}), f32[768,96]{0,1:T(8,128)}) %reduce-scatter.17.cloned.1.call-update) | async-done | bytes 294928 | tf_op jit(solution)/shard_map/reduce_scatter | solution.py:319
  1571.4 36.0 %reduce-scatter.21.cloned.1.call-done = f32[96,2]{1,0:T(8,128)} async-done(((f32[768,2]{1,0:T(8,128)}), f32[96,2]{1,0:T(8,128)}) %reduce-scatter.21.cloned.1.call-update) | async-done | bytes 784
  1609.5 36.4 %reduce-scatter.19.cloned.1.call-done = f32[96,192]{1,0:T(8,128)} async-done(((f32[768,192]{1,0:T(8,128)}), f32[96,192]{1,0:T(8,128)}) %reduce-scatter.19.cloned.1.call-update) | async-done | bytes 73744
  1647.4 56.6 %reduce-scatter.15.cloned.1.call-done = f32[96,2,768]{2,0,1:T(8,128)} async-done(((f32[768,2,768]{2,0,1:T(8,128)}), f32[96,2,768]{2,0,1:T(8,128)}) %reduce-scatter.15.cloned.1.call-update) | async-done | bytes 589840 | tf_op jit(solution)/shard_map/reduce_scatter | solution.py:318
  1705.9 44.6 %reduce-scatter.13.cloned.1.call-done = f32[96,3,192]{2,0,1:T(8,128)} async-done(((f32[768,3,192]{2,0,1:T(8,128)}), f32[96,3,192]{2,0,1:T(8,128)}) %reduce-scatter.13.cloned.1.call-update) | async-done | bytes 221200 | tf_op jit(solution)/shard_map/reduce_scatter | solution.py:316
  1759.1 13.3 copy.158
  1772.5 53.5 %psum.39 = f32[]{:T(128)} all-reduce(f32[]{:T(128)S(6)} %add.324), channel_id=1, replica_groups=mesh['batch'=8,'mp'=4] {'batch','mp'}, use_global_device_ids=true, to_apply=%region_46.47 | all-reduce | flops 1 | bytes 8 | tf_op jit(solution)/shard_map/psum | solution.py:326
  1835.5 123.4 %all-gather.11.cloned.1.call-done = f32[3816,768]{0,1:T(8,128)} async-done(((f32[3816,192]{0,1:T(8,128)}), f32[3816,768]{0,1:T(8,128)}) %all-gather.11.cloned.1.call-update) | async-done | bytes 11722768 | tf_op jit(solution)/shard_map/all_gather | solution.py:325
  1958.9 17.3 fusion.46
  1976.2 12.3 copy.169
  1988.5 22.2 %fusion.45 = f32[3816,768]{0,1:T(8,128)} fusion(f32[3816,768]{0,1:T(8,128)} %copy.141, f32[3816,768]{0,1:T(8,128)} %get-tuple-element.440, f32[3816,768]{0,1:T(8,128)} %copy.158, f32[3816,768]{0,1:T(8,128)} %copy.160), kind=kLoop, calls=%fused_computation.57 | loop fusion | flops 41029632 | bytes 58613760 | tf_op jit(solution)/shard_map/sub | solution.py:170
  2010.8 12.3 copy.167
  2023.1 12.4 copy.171
  (362 shorter events, 386.2 us)
Async XLA Ops:
  7.2 97.2 %copy-start = (s32[30528]{0:T(1024)S(1)}, s32[30528]{0:T(1024)}, u32[]{:S(2)}) copy-start(s32[30528]{0:T(1024)} %param.32) | copy-start | bytes 366340
  7.2 316.0 %all-gather.13.cloned.1.call-start = ((), (), s32[]{:S(2)}) async-start(), calls=%async_computation.17 | async-start | bytes 2949120 | tf_op jit(solution)/shard_map/all_gather | solution.py:218
  21.7 3.4 collective-permute-start
  28.9 67.2 %collective-permute-start.1 = (bf16[2,3816,192]{1,2,0:T(8,128)(2,1)S(1)}, bf16[2,3816,192]{1,2,0:T(8,128)(2,1)}, u32[]{:S(2)}, u32[]{:S(2)}) collective-permute-start(bf16[2,3816,192]{1,2,0:T(8,128)(2,1)S(1)} %pad_maximum_fusion.2), channel_id=1, source_target_pairs={{0,8},{4,12},{8,0},{12,4},{16,24},{20,28},{24,16},{28,20},{1,9},{5... | collective-permute-start | bytes 8792072 | tf_op jit(solution)/shard_map/ppermute | solution.py:28
  102.6 128.9 %collective-permute-start.2 = (bf16[4,3816,192]{1,2,0:T(8,128)(2,1)}, bf16[4,3816,192]{1,2,0:T(8,128)(2,1)}, u32[]{:S(2)}, u32[]{:S(2)}) collective-permute-start(bf16[4,3816,192]{1,2,0:T(8,128)(2,1)} %pad_maximum_fusion.1), channel_id=1, source_target_pairs={{0,16},{4,20},{8,24},{12,28},{16,0},{20,4},{24,8},{28,12},{1,17},{... | collective-permute-start | bytes 17584136 | tf_op jit(solution)/shard_map/ppermute | solution.py:28
  112.8 123.1 %copy-start.52 = (s32[1536]{0:T(1024)}, s32[1536]{0:T(1024)S(1)}, u32[]{:S(2)}) copy-start(s32[1536]{0:T(1024)S(1)} %fusion.104) | copy-start | bytes 18436
  271.4 104.6 %all-gather.7.cloned.1.call-start = ((), (), s32[]{:S(2)}) async-start(), calls=%async_computation.7 | async-start | bytes 2654208 | tf_op jit(solution)/shard_map/all_gather | solution.py:207
  272.2 264.9 %all-reduce.11.cloned.1.call-start = ((), (), s32[]{:S(2)}) async-start(), calls=%async_computation.6 | async-start | bytes 9437184 | tf_op jit(solution)/shard_map/psum | solution.py:233
  297.3 65.8 %copy-start.13 = (bf16[192,768]{0,1:T(8,128)(2,1)}, bf16[192,768]{0,1:T(8,128)(2,1)S(1)}, u32[]{:S(2)}) copy-start(bf16[192,768]{0,1:T(8,128)(2,1)S(1)} %all_gather.26) | copy-start | bytes 884740
  366.2 196.3 %all-gather.9.cloned.1.call-start = ((), (), s32[]{:S(2)}) async-start(), calls=%async_computation.8 | async-start | bytes 1327104 | tf_op jit(solution)/shard_map/all_gather | solution.py:208
  366.9 373.9 %all-reduce.13.cloned.1.call-start = ((), (), s32[]{:S(2)}) async-start(), calls=%async_computation.9 | async-start | bytes 9437184 | tf_op jit(solution)/shard_map/psum | solution.py:241
  376.0 585.8 %copy-start.48 = (f32[768]{0:T(1024)}, f32[768]{0:T(1024)S(1)}, u32[]{:S(2)}) copy-start(f32[768]{0:T(1024)S(1)} %get-tuple-element.396) | copy-start | bytes 9220
  541.1 420.7 %copy-start.44 = (f32[1536]{0:T(1024)}, f32[1536]{0:T(1024)S(1)}, u32[]{:S(2)}) copy-start(f32[1536]{0:T(1024)S(1)} %broadcast_multiply_fusion.3) | copy-start | bytes 18436
  541.6 420.1 %copy-start.46 = (f32[1536]{0:T(1024)}, f32[1536]{0:T(1024)S(1)}, u32[]{:S(2)}) copy-start(f32[1536]{0:T(1024)S(1)} %fusion.101) | copy-start | bytes 18436
  568.7 382.4 %all-reduce.15.cloned.1.call-start = ((), (), s32[]{:S(2)}) async-start(), calls=%async_computation.10 | async-start | bytes 9437184 | tf_op jit(solution)/shard_map/psum | solution.py:281
  765.3 185.8 %copy-start.50 = (f32[1536]{0:T(1024)}, f32[1536]{0:T(1024)S(1)}, u32[]{:S(2)}) copy-start(f32[1536]{0:T(1024)S(1)} %negate_multiply_fusion.1) | copy-start | bytes 18436
  780.9 530.8 %all-reduce.17.cloned.1.call-start = ((), (), s32[]{:S(2)}) async-start(), calls=%async_computation.11 | async-start | bytes 9437184 | tf_op jit(solution)/shard_map/psum | solution.py:306
  969.1 163.9 %copy-start.23 = (f32[1536,32]{0,1:T(8,128)S(1)}, f32[1536,32]{0,1:T(8,128)}, u32[]{:S(2)}) copy-start(f32[1536,32]{0,1:T(8,128)} %copy-done.22) | copy-start | bytes 589828
  1140.6 383.2 %reduce-scatter.11.cloned.1.call-start = ((), (), s32[]{:S(2)}) async-start(), calls=%async_computation.12 | async-start | bytes 35168256 | tf_op jit(solution)/shard_map/reduce_scatter | solution.py:315
  1335.2 234.5 %reduce-scatter.17.cloned.1.call-start = ((), (), s32[]{:S(2)}) async-start(), calls=%async_computation.15 | async-start | bytes 2654208 | tf_op jit(solution)/shard_map/reduce_scatter | solution.py:319
  1342.6 264.7 %reduce-scatter.21.cloned.1.call-start = ((), (), s32[]{:S(2)}) async-start(), calls=%async_computation.19 | async-start | bytes 442368
  1343.7 302.1 %reduce-scatter.19.cloned.1.call-start = ((), (), s32[]{:S(2)}) async-start(), calls=%async_computation.18 | async-start | bytes 884736
  1349.4 354.7 %reduce-scatter.15.cloned.1.call-start = ((), (), s32[]{:S(2)}) async-start(), calls=%async_computation.14 | async-start | bytes 5308416 | tf_op jit(solution)/shard_map/reduce_scatter | solution.py:318
  1364.8 385.7 %reduce-scatter.13.cloned.1.call-start = ((), (), s32[]{:S(2)}) async-start(), calls=%async_computation.13 | async-start | bytes 2654208 | tf_op jit(solution)/shard_map/reduce_scatter | solution.py:316
  1372.4 586.5 %all-gather.11.cloned.1.call-start = ((), (), s32[]{:S(2)}) async-start(), calls=%async_computation.16 | async-start | bytes 14745600 | tf_op jit(solution)/shard_map/all_gather | solution.py:325
  1759.1 67.6 %copy-start.16 = (f32[96,2,768]{2,1,0:T(2,128)S(1)}, f32[96,2,768]{2,1,0:T(2,128)}, u32[]{:S(2)}) copy-start(f32[96,2,768]{2,1,0:T(2,128)} %param.37) | copy-start | bytes 1769476
  1759.1 67.6 %copy-start.17 = (f32[96,2,768]{2,0,1:T(8,128)S(1)}, f32[96,2,768]{2,0,1:T(8,128)}, u32[]{:S(2)}) copy-start(f32[96,2,768]{2,0,1:T(8,128)} %reduce-scatter.15.cloned.1.call-done) | copy-start | bytes 1769476
  1759.1 67.6 %copy-start.34 = (f32[96,2,768]{2,1,0:T(2,128)S(1)}, f32[96,2,768]{2,1,0:T(2,128)}, u32[]{:S(2)}) copy-start(f32[96,2,768]{2,1,0:T(2,128)} %param.43) | copy-start | bytes 1769476
  1759.1 67.6 %copy-start.35 = (f32[96,2,768]{2,1,0:T(2,128)S(1)}, f32[96,2,768]{2,1,0:T(2,128)}, u32[]{:S(2)}) copy-start(f32[96,2,768]{2,1,0:T(2,128)} %param.49) | copy-start | bytes 1769476
  1772.4 60.9 %copy-start.27 = (f32[768,96]{0,1:T(8,128)S(1)}, f32[768,96]{0,1:T(8,128)}, u32[]{:S(2)}) copy-start(f32[768,96]{0,1:T(8,128)} %param.38) | copy-start | bytes 884740
  1772.4 60.9 %copy-start.30 = (f32[768,96]{0,1:T(8,128)S(1)}, f32[768,96]{0,1:T(8,128)}, u32[]{:S(2)}) copy-start(f32[768,96]{0,1:T(8,128)} %reduce-scatter.17.cloned.1.call-done) | copy-start | bytes 884740
  1772.5 60.9 %copy-start.40 = (f32[768,96]{0,1:T(8,128)S(1)}, f32[768,96]{0,1:T(8,128)}, u32[]{:S(2)}) copy-start(f32[768,96]{0,1:T(8,128)} %param.44) | copy-start | bytes 884740
  (58 other events, 575.9 us)
Sparse Core Ops, SparseCore 0:
  271.5 51.6 all-gather.12
  325.7 27.8 all-gather.6
  366.3 170.7 all-reduce.10
  539.4 23.0 all-gather.8
  568.8 171.9 all-reduce.12
  781.0 170.0 all-reduce.14
  1140.7 170.9 all-reduce.16
  1335.3 188.4 reduce-scatter.10
  1527.2 42.5 reduce-scatter.16
  1573.5 33.7 reduce-scatter.20
  1610.8 34.9 reduce-scatter.18
  1650.1 53.8 reduce-scatter.14
  1707.9 42.4 reduce-scatter.12
  1752.5 206.2 all-gather.10
